TPU v7x, 32 devices: a whole 2x2x4 slice. The times are simulated.
32 devices in a mesh: groups: 2 (over x), ctx: 16 (over z, y, core).
Axes of the slice: x: 2, y: 2, z: 4, core: 2. Of those that a mesh axis runs over, the one named last changes fastest.
Arguments:
- queries: bfloat16 [8192, 1024], P(('groups', 'ctx')), parts along dimension 0, may hold values from -128 to 128
- keys: bfloat16 [8192, 128], P(('groups', 'ctx')), parts along dimension 0, may hold values from -32 to 32
- values: bfloat16 [8192, 128], P(('groups', 'ctx')), parts along dimension 0, may hold values from -6 to 6
- doc_ids: int32 [8192], P(('groups', 'ctx')), parts along dimension 0, may hold values from 0 to 2, never falling along the last dimension, each value on 1 to 3072 neighbouring positions
Outputs:
- attended: bfloat16 [8192, 1024], P(('groups', 'ctx')), parts along dimension 0
There are 2 independent parts, one for each index of `groups`. A program takes and returns all parts, laid end to end along the dimension named above; each array names one. Nothing has to cross between parts.
All inputs are finite; a program needn't handle non-finite values.
Results may differ from a plain program's by a relative error of at most 0.0041.
Values may be sent and summed in bfloat16 or wider, within the bound.
A program may use at most 64 MiB of HBM per device.

v0:
```python
from functools import partial

import jax
import jax.numpy as jnp
from jax import lax
from jax.sharding import PartitionSpec as P

FLOOR_SCORE = -1e30
LARGEST_BLOCK = 2048


def attend_block(
    state,
    query_rows,
    query_place,
    query_doc,
    key_block,
    value_block,
    doc_block,
    place_block,
    score_scale,
):
    running_max, weight_sum, weighted = state
    token_count, head_count = running_max.shape
    block_rows = key_block.shape[0]
    scores = (
        lax.dot_general(
            query_rows, key_block, (((1,), (1,)), ((), ())), preferred_element_type=jnp.float32
        )
        * score_scale
    )
    scores = scores.reshape(token_count, head_count, block_rows)
    visible = (place_block[None, :] <= query_place[:, None]) & (
        doc_block[None, :] == query_doc[:, None]
    )
    visible = visible[:, None, :]
    block_max = jnp.max(jnp.where(visible, scores, FLOOR_SCORE), axis=2)
    new_max = jnp.maximum(running_max, block_max)
    weights = jnp.where(visible, jnp.exp(scores - new_max[:, :, None]), 0.0)
    factor = jnp.exp(running_max - new_max)
    weight_sum = weight_sum * factor + jnp.sum(weights, axis=2)
    flat_weights = weights.reshape(token_count * head_count, block_rows).astype(jnp.bfloat16)
    weighted = weighted * factor.reshape(-1)[:, None] + jnp.dot(
        flat_weights, value_block, preferred_element_type=jnp.float32
    )
    return (new_max, weight_sum, weighted)


def keep_state(state):
    return state


def on_device(queries, keys, values, doc_ids):
    place = lax.axis_index("ctx")
    local_rows = queries.shape[0]
    half_rows = local_rows // 2
    head_dim = keys.shape[1]
    head_count = queries.shape[1] // head_dim
    score_scale = head_dim ** (-0.5)
    row_index = jnp.arange(local_rows, dtype=jnp.int32)
    held_query, held_doc = (queries, doc_ids)
    row_place = place * local_rows + row_index
    slots = []
    for slot_number in range(2):
        first = slot_number * half_rows
        query_half = held_query[first : first + half_rows]
        doc_half = held_doc[first : first + half_rows]
        place_half = row_place[first : first + half_rows]
        query_rows = query_half.reshape(half_rows * head_count, head_dim)
        slots.append((query_rows, place_half, doc_half, jnp.max(place_half)))
    empty_state = (
        jnp.full((half_rows, head_count), FLOOR_SCORE, jnp.float32),
        jnp.zeros((half_rows, head_count), jnp.float32),
        jnp.zeros((half_rows * head_count, head_dim), jnp.float32),
    )
    init_state = (empty_state, empty_state)
    state_all = init_state
    key_piece = lax.all_gather(keys, "ctx", axis=0, tiled=True)
    value_piece = lax.all_gather(values, "ctx", axis=0, tiled=True)
    doc_piece = lax.all_gather(doc_ids, "ctx", axis=0, tiled=True)
    piece_count = key_piece.shape[0]
    block_rows = min(piece_count, LARGEST_BLOCK)
    block_count = piece_count // block_rows
    places = jnp.arange(piece_count, dtype=jnp.int32).reshape(block_count, block_rows)
    stacked = (
        key_piece.reshape(block_count, block_rows, head_dim),
        value_piece.reshape(block_count, block_rows, head_dim),
        doc_piece.reshape(block_count, block_rows),
        places,
    )

    def advance(states, block_data):
        key_block, value_block, doc_block, place_block = block_data
        nearest = jnp.min(place_block)
        updated = []
        for slot_number in range(2):
            query_rows, query_place, query_doc, last_place = slots[slot_number]
            work = partial(
                attend_block,
                query_rows=query_rows,
                query_place=query_place,
                query_doc=query_doc,
                key_block=key_block,
                value_block=value_block,
                doc_block=doc_block,
                place_block=place_block,
                score_scale=score_scale,
            )
            updated.append(lax.cond(nearest <= last_place, work, keep_state, states[slot_number]))
        return (tuple(updated), None)

    state_all, unused = lax.scan(advance, state_all, stacked)
    outputs = []
    for slot_number in range(2):
        running_max, weight_sum, weighted = state_all[slot_number]
        outputs.append(
            (weighted / weight_sum.reshape(-1)[:, None])
            .astype(jnp.bfloat16)
            .reshape(half_rows, head_count * head_dim)
        )
    result = jnp.concatenate(outputs, axis=0)
    return result


def solution(mesh):
    return jax.shard_map(
        on_device,
        mesh=mesh,
        in_specs=(
            P(("groups", "ctx"), None),
            P(("groups", "ctx"), None),
            P(("groups", "ctx"), None),
            P(("groups", "ctx")),
        ),
        out_specs=P(("groups", "ctx"), None),
        check_vma=False,
    )
```

profile of v0, /device:TPU:24, one launch (start us, length us, event | category | flops | bytes accessed | tf_op | source)
XLA Modules:
  0.0 163.5 jit_solution(13296015748481120245)
XLA Ops:
  8.0 17.1 %all-gather = s32[16,1,256]{2,1,0:T(1,128)S(1)} all-gather(s32[1,1,256]{2,1,0:T(1,128)} %bitcast.51), channel_id=1, replica_groups=mesh['groups'=2,'ctx'=16] {'ctx'}, dimensions={0}, use_global_device_ids=true | all-gather | bytes 17408 | tf_op jit(solution)/shard_map/all_gather | solution.py:80
  25.2 1.1 fusion.23
  26.5 1.5 slice_reduce_fusion
  28.0 19.4 %all-gather.4.cloned.1.call-done = bf16[4096,128]{1,0:T(8,128)(2,1)} async-done(((bf16[256,128]{1,0:T(8,128)(2,1)}), bf16[4096,128]{1,0:T(8,128)(2,1)}) %all-gather.4.cloned.1.call-update) | async-done | bytes 1048592 | tf_op jit(solution)/shard_map/all_gather | solution.py:78
  47.3 39.0 %all-gather.6.cloned.1.call-done = bf16[4096,128]{1,0:T(8,128)(2,1)} async-done(((bf16[256,128]{1,0:T(8,128)(2,1)}), bf16[4096,128]{1,0:T(8,128)(2,1)}) %all-gather.6.cloned.1.call-update) | async-done | bytes 1048592 | tf_op jit(solution)/shard_map/all_gather | solution.py:79
  86.5 68.5 %while.20 = (s32[]{:T(128)}, f32[128,8]{1,0:T(8,128)S(1)}, f32[128,8]{1,0:T(8,128)S(1)}, f32[1024,128]{1,0:T(8,128)S(1)}, f32[128,8]{1,0:T(8,128)S(1)}, /*index=...) while((s32[]{:T(128)}, f32[128,8]{1,0:T(8,128)S(1)}, ...), condition=%wide.region_12.13_spmd, body=%wide.region_2.12_spmd.sunk | while | flops 2195724288 | bytes 59509236 | solution.py:112
  89.9 1.3 dynamic-slice_bitcast_fusion.3
  91.1 14.8 %conditional.4 = ((f32[128,8]{1,0:T(8,128)S(1)}, f32[128,8]{1,0:T(8,128)S(1)}, f32[1024,128]{1,0:T(8,128)S(1)})) conditional(s32[]{:T(128)} %convert_element_type.32, (f32[128,8]{1,0:T(8,128)S(1)}, f32[128,8]{1,0:T(8,128)S(1)}, f32[1024,128]{1,0:T(8,128)S(1)}) %tuple.54, (s32[2048]{0:T(1024)S(1)}, s32[128]{0:T(128)S(1)}, s32[2048]{0:T(1024)S(1)}, ...), branch_computations={%region_4.4_spmd, %region_5.7_spmd} | conditional | flops 1097861120 | bytes 28689440 | solution.py:109
  91.4 4.3 %fusion = (f32[1024]{0:T(1024)S(1)}, f32[1024,2048]{1,0:T(8,128)}) fusion(pred[128,2048]{1,0:T(8,128)(4,1)S(1)} %compare_and_fusion, bf16[1024,128]{1,0:T(8,128)(2,1)S(1)} %get-tuple-element.138, bf16[2048,128]{1,0:T(8,128)(2,1)S(1)} %get-tuple-element.139), kind=kOutput, calls=%fused_computation.2 | convolution fusion | flops 543161344 | bytes 9441280 | tf_op jit(solution)/shard_map/while/body/eval_jaxpr/cond/branch_1_fun/dot_general | solution.py:27
  95.9 4.9 %fusion.2 = f32[1024]{0:T(1024)S(1)} fusion(f32[1024,2048]{1,0:T(8,128)} %get-tuple-element.234, f32[1024]{0:T(1024)S(1)} %sub.23, pred[128,2048]{1,0:T(8,128)(4,1)S(1)} %compare_and_fusion), kind=kLoop, calls=%fused_computation.4 | loop fusion | flops 8387584 | bytes 8658944 | tf_op jit(solution)/shard_map/while/body/eval_jaxpr/cond/branch_1_fun/reduce_sum | solution.py:41
  101.1 4.8 %fusion.6 = f32[1024,128]{1,0:T(8,128)S(1)} fusion(bf16[2048,128]{1,0:T(8,128)(2,1)S(1)} %get-tuple-element.142, f32[1024,2048]{1,0:T(8,128)} %get-tuple-element.234, f32[1024]{0:T(1024)S(1)} %sub.23, pred[128,2048]{1,0:T(8,128)(4,1)S(1)} %compare_and_fusion, f32[1024,128]{1,0:T(8,128)S(1)} %get-tuple-element.141, f32[1024]{0:T(1024)S(1)} %mul.26), kind=kOutput, calls=%fused_computation.7 | convolution fusion | flops 545521664 | bytes 10231808 | tf_op jit(solution)/shard_map/while/body/eval_jaxpr/cond/branch_1_fun/dot_general | solution.py:43
  105.9 14.8 %conditional.5 = ((f32[128,8]{1,0:T(8,128)S(1)}, f32[128,8]{1,0:T(8,128)S(1)}, f32[1024,128]{1,0:T(8,128)S(1)})) conditional(s32[]{:T(128)} %convert_element_type.33, (f32[128,8]{1,0:T(8,128)S(1)}, f32[128,8]{1,0:T(8,128)S(1)}, f32[1024,128]{1,0:T(8,128)S(1)}) %tuple.56, (s32[2048]{0:T(1024)S(1)}, s32[128]{0:T(128)S(1)}, s32[2048]{0:T(1024)S(1)}, ...), branch_computations={%region_8.8_spmd, %region_9.11_spmd} | conditional | flops 1097861120 | bytes 28689440 | solution.py:109
  106.2 4.3 %fusion.11 = (f32[1024]{0:T(1024)S(1)}, f32[1024,2048]{1,0:T(8,128)}) fusion(pred[128,2048]{1,0:T(8,128)(4,1)S(1)} %compare_and_fusion.1, bf16[1024,128]{1,0:T(8,128)(2,1)S(1)} %get-tuple-element.148, bf16[2048,128]{1,0:T(8,128)(2,1)S(1)} %get-tuple-element.149), kind=kOutput, calls=%fused_computation.15 | convolution fusion | flops 543161344 | bytes 9441280 | tf_op jit(solution)/shard_map/while/body/eval_jaxpr/cond/branch_1_fun/dot_general | solution.py:27
  110.7 4.9 %fusion.13 = f32[1024]{0:T(1024)S(1)} fusion(f32[1024,2048]{1,0:T(8,128)} %get-tuple-element.236, f32[1024]{0:T(1024)S(1)} %sub.27, pred[128,2048]{1,0:T(8,128)(4,1)S(1)} %compare_and_fusion.1), kind=kLoop, calls=%fused_computation.17 | loop fusion | flops 8387584 | bytes 8658944 | tf_op jit(solution)/shard_map/while/body/eval_jaxpr/cond/branch_1_fun/reduce_sum | solution.py:41
  115.9 4.8 %fusion.17 = f32[1024,128]{1,0:T(8,128)S(1)} fusion(bf16[2048,128]{1,0:T(8,128)(2,1)S(1)} %get-tuple-element.152, f32[1024,2048]{1,0:T(8,128)} %get-tuple-element.236, f32[1024]{0:T(1024)S(1)} %sub.27, pred[128,2048]{1,0:T(8,128)(4,1)S(1)} %compare_and_fusion.1, f32[1024,128]{1,0:T(8,128)S(1)} %get-tuple-element.151, f32[1024]{0:T(1024)S(1)} %mul.31), kind=kOutput, calls=%fused_computation.20 | convolution fusion | flops 545521664 | bytes 10231808 | tf_op jit(solution)/shard_map/while/body/eval_jaxpr/cond/branch_1_fun/dot_general | solution.py:43
  124.1 1.3 dynamic-slice_bitcast_fusion.3
  125.4 14.8 %conditional.4 = ((f32[128,8]{1,0:T(8,128)S(1)}, f32[128,8]{1,0:T(8,128)S(1)}, f32[1024,128]{1,0:T(8,128)S(1)})) conditional(s32[]{:T(128)} %convert_element_type.32, (f32[128,8]{1,0:T(8,128)S(1)}, f32[128,8]{1,0:T(8,128)S(1)}, f32[1024,128]{1,0:T(8,128)S(1)}) %tuple.54, (s32[2048]{0:T(1024)S(1)}, s32[128]{0:T(128)S(1)}, s32[2048]{0:T(1024)S(1)}, ...), branch_computations={%region_4.4_spmd, %region_5.7_spmd} | conditional | flops 1097861120 | bytes 28689440 | solution.py:109
  125.7 4.3 %fusion = (f32[1024]{0:T(1024)S(1)}, f32[1024,2048]{1,0:T(8,128)}) fusion(pred[128,2048]{1,0:T(8,128)(4,1)S(1)} %compare_and_fusion, bf16[1024,128]{1,0:T(8,128)(2,1)S(1)} %get-tuple-element.138, bf16[2048,128]{1,0:T(8,128)(2,1)S(1)} %get-tuple-element.139), kind=kOutput, calls=%fused_computation.2 | convolution fusion | flops 543161344 | bytes 9441280 | tf_op jit(solution)/shard_map/while/body/eval_jaxpr/cond/branch_1_fun/dot_general | solution.py:27
  130.1 4.9 %fusion.2 = f32[1024]{0:T(1024)S(1)} fusion(f32[1024,2048]{1,0:T(8,128)} %get-tuple-element.234, f32[1024]{0:T(1024)S(1)} %sub.23, pred[128,2048]{1,0:T(8,128)(4,1)S(1)} %compare_and_fusion), kind=kLoop, calls=%fused_computation.4 | loop fusion | flops 8387584 | bytes 8658944 | tf_op jit(solution)/shard_map/while/body/eval_jaxpr/cond/branch_1_fun/reduce_sum | solution.py:41
  135.3 4.8 %fusion.6 = f32[1024,128]{1,0:T(8,128)S(1)} fusion(bf16[2048,128]{1,0:T(8,128)(2,1)S(1)} %get-tuple-element.142, f32[1024,2048]{1,0:T(8,128)} %get-tuple-element.234, f32[1024]{0:T(1024)S(1)} %sub.23, pred[128,2048]{1,0:T(8,128)(4,1)S(1)} %compare_and_fusion, f32[1024,128]{1,0:T(8,128)S(1)} %get-tuple-element.141, f32[1024]{0:T(1024)S(1)} %mul.26), kind=kOutput, calls=%fused_computation.7 | convolution fusion | flops 545521664 | bytes 10231808 | tf_op jit(solution)/shard_map/while/body/eval_jaxpr/cond/branch_1_fun/dot_general | solution.py:43
  140.2 14.8 %conditional.5 = ((f32[128,8]{1,0:T(8,128)S(1)}, f32[128,8]{1,0:T(8,128)S(1)}, f32[1024,128]{1,0:T(8,128)S(1)})) conditional(s32[]{:T(128)} %convert_element_type.33, (f32[128,8]{1,0:T(8,128)S(1)}, f32[128,8]{1,0:T(8,128)S(1)}, f32[1024,128]{1,0:T(8,128)S(1)}) %tuple.56, (s32[2048]{0:T(1024)S(1)}, s32[128]{0:T(128)S(1)}, s32[2048]{0:T(1024)S(1)}, ...), branch_computations={%region_8.8_spmd, %region_9.11_spmd} | conditional | flops 1097861120 | bytes 28689440 | solution.py:109
  140.5 4.3 %fusion.11 = (f32[1024]{0:T(1024)S(1)}, f32[1024,2048]{1,0:T(8,128)}) fusion(pred[128,2048]{1,0:T(8,128)(4,1)S(1)} %compare_and_fusion.1, bf16[1024,128]{1,0:T(8,128)(2,1)S(1)} %get-tuple-element.148, bf16[2048,128]{1,0:T(8,128)(2,1)S(1)} %get-tuple-element.149), kind=kOutput, calls=%fused_computation.15 | convolution fusion | flops 543161344 | bytes 9441280 | tf_op jit(solution)/shard_map/while/body/eval_jaxpr/cond/branch_1_fun/dot_general | solution.py:27
  144.9 4.9 %fusion.13 = f32[1024]{0:T(1024)S(1)} fusion(f32[1024,2048]{1,0:T(8,128)} %get-tuple-element.236, f32[1024]{0:T(1024)S(1)} %sub.27, pred[128,2048]{1,0:T(8,128)(4,1)S(1)} %compare_and_fusion.1), kind=kLoop, calls=%fused_computation.17 | loop fusion | flops 8387584 | bytes 8658944 | tf_op jit(solution)/shard_map/while/body/eval_jaxpr/cond/branch_1_fun/reduce_sum | solution.py:41
  150.1 4.8 %fusion.17 = f32[1024,128]{1,0:T(8,128)S(1)} fusion(bf16[2048,128]{1,0:T(8,128)(2,1)S(1)} %get-tuple-element.152, f32[1024,2048]{1,0:T(8,128)} %get-tuple-element.236, f32[1024]{0:T(1024)S(1)} %sub.27, pred[128,2048]{1,0:T(8,128)(4,1)S(1)} %compare_and_fusion.1, f32[1024,128]{1,0:T(8,128)S(1)} %get-tuple-element.151, f32[1024]{0:T(1024)S(1)} %mul.31), kind=kOutput, calls=%fused_computation.20 | convolution fusion | flops 545521664 | bytes 10231808 | tf_op jit(solution)/shard_map/while/body/eval_jaxpr/cond/branch_1_fun/dot_general | solution.py:43
  (57 shorter events, 7.7 us)
Async XLA Ops:
  6.5 40.8 %all-gather.4.cloned.1.call-start = ((), (), s32[]{:S(2)}) async-start(), calls=%async_computation | async-start | bytes 1114112 | tf_op jit(solution)/shard_map/all_gather | solution.py:78
  7.3 79.1 %all-gather.6.cloned.1.call-start = ((), (), s32[]{:S(2)}) async-start(), calls=%async_computation.1 | async-start | bytes 1114112 | tf_op jit(solution)/shard_map/all_gather | solution.py:79
Sparse Core Ops, SparseCore 0:
  9.5 37.8 all-gather.3
  49.5 36.8 all-gather.5
where the time goes:
time: 164 us
  waiting for transfers between devices  59.8 us (36%)
  matrix products  36.4 us (22%)
  other arithmetic  25.3 us (15%)
  blocking collectives  17.1 us (10%)
  between operations  13.5 us (8%)
  local copies, waits for them, and re-layouts  5.78 us (4%)
  loops' own time  5.57 us (3%)
    all_gather x1, waiting for transfers between devices, on_device(): value_piece = lax.all_gather(values, 'ctx', axis=0, tiled=True)  39 us
    reduce_sum x4, other arithmetic, attend_block(): weight_sum = weight_sum * factor + jnp.sum(weights, axis=2)  19.8 us
    all_gather x1, waiting for transfers between devices, on_device(): key_piece = lax.all_gather(keys, 'ctx', axis=0, tiled=True)  19.4 us
    dot_general x4, matrix products, attend_block(): jnp.dot(flat_weights, value_block, preferred_element_type=jnp.float32)  19.3 us
    all_gather x1, blocking collectives, on_device(): doc_piece = lax.all_gather(doc_ids, 'ctx', axis=0, tiled=True)  17.1 us
    dot_general x4, matrix products, attend_block(): lax.dot_general(query_rows, key_block, (((1,), (1,)), ((), ())), preferre...  17.1 us
    another operation x1, loops' own time, on_device(): state_all, unused = lax.scan(advance, state_all, stacked)  5.28 us
  transfers between devices with their start and end apart: 2, of which 2 were waited for; matrix products, arithmetic and copies ran while one was open for 2% of the time, Pallas kernels for 0%

commit v1 on v0

v1 whole, which is shorter than its diff:
```python
import functools

import jax
import jax.numpy as jnp
from jax import lax
from jax.experimental import pallas as pl
from jax.experimental.pallas import tpu as pltpu
from jax.sharding import PartitionSpec as P

HIDDEN = -1e30
LOG2E = 1.4426950408889634


def kernel(
    n,
    q_ref,
    k_hbm,
    v_hbm,
    d_hbm,
    o_ref,
    kv,
    docs,
    bias,
    m_ref,
    l_ref,
    acc_ref,
    fill_sem,
    send_kv,
    send_doc,
    recv_kv,
    recv_doc,
):
    rows, width = q_ref.shape
    dim = k_hbm.shape[1]
    heads = width // dim
    levels = n // 4
    window = 3 * n // 4
    me = lax.axis_index("ctx")
    z = me // 4
    r = me % 4
    y = r // 2
    c = r % 2
    up = me + 4
    across = z * 4 + (1 - y) * 2 + c
    partner = z * 4 + y * 2 + (1 - c)
    scale = dim ** (-0.5) * LOG2E

    def span(block):
        return pl.ds(pl.multiple_of(block * rows, rows), rows)

    fills = [
        pltpu.make_async_copy(k_hbm, kv.at[0, span(me), :], fill_sem.at[0]),
        pltpu.make_async_copy(v_hbm, kv.at[1, span(me), :], fill_sem.at[1]),
        pltpu.make_async_copy(d_hbm, docs.at[me], fill_sem.at[2]),
    ]
    for fill in fills:
        fill.start()

    barrier = pltpu.get_barrier_semaphore()

    def greet(device):
        pl.semaphore_signal(
            barrier, inc=1, device_id={"ctx": device}, device_id_type=pl.DeviceIdType.MESH
        )

    greet(partner)
    greet(across)

    @pl.when(z > 0)
    def _():
        greet(me - 4)

    @pl.when(z < levels - 1)
    def _():
        greet(up)

    pl.semaphore_wait(barrier, 2 + jnp.minimum(z, 1) + jnp.minimum(levels - 1 - z, 1))

    for fill in fills:
        fill.wait()

    def copies(stream, slot, block, device):
        return (
            pltpu.make_async_remote_copy(
                src_ref=kv.at[:, span(block), :],
                dst_ref=kv.at[:, span(block), :],
                send_sem=send_kv.at[stream, slot],
                recv_sem=recv_kv.at[stream, slot],
                device_id={"ctx": device},
                device_id_type=pl.DeviceIdType.MESH,
            ),
            pltpu.make_async_remote_copy(
                src_ref=docs.at[block],
                dst_ref=docs.at[block],
                send_sem=send_doc.at[stream, slot],
                recv_sem=recv_doc.at[stream, slot],
                device_id={"ctx": device},
                device_id_type=pl.DeviceIdType.MESH,
            ),
        )

    def start(stream, slot, block, device):
        for copy in copies(stream, slot, block, device):
            copy.start()

    def arrived(stream, slot, block, device):
        for copy in copies(stream, slot, block, device):
            copy.wait_recv()

    def sent(stream, slot, block, device):
        for copy in copies(stream, slot, block, device):
            copy.wait_send()

    def relay(level):
        block = level * 4 + r

        @pl.when(z < levels - 1)
        def _():
            start(0, level, block, up)

        start(1, level, block, across)
        start(2, level, block, partner)

    m_ref[...] = jnp.full_like(m_ref, HIDDEN)
    l_ref[...] = jnp.zeros_like(l_ref)
    acc_ref[...] = jnp.zeros_like(acc_ref)
    doc_col = jnp.broadcast_to(docs[me], (dim, rows)).T
    relay(z)

    def process(chunk):
        @pl.when((chunk <= me // 2) & (chunk * 2 + 1 >= me - window))
        def _():
            row_id = me * rows + lax.broadcasted_iota(jnp.int32, (rows, dim), 0)
            lane = lax.broadcasted_iota(jnp.int32, (rows, dim), 1)
            for half in range(2):
                doc_row = docs[chunk * 2 + half]
                for part in range(rows // dim):
                    key_id = (chunk * 2 + half) * rows + part * dim + lane
                    same = doc_row[:, part * dim : (part + 1) * dim] == doc_col
                    bias[:, pl.ds(half * rows + part * dim, dim)] = jnp.where(
                        same & (key_id <= row_id), 0.0, HIDDEN
                    )
            place = pl.ds(pl.multiple_of(chunk * 2 * rows, 2 * rows), 2 * rows)
            for head in range(heads):
                cols = slice(head * dim, (head + 1) * dim)
                s = (
                    lax.dot_general(
                        q_ref[:, cols],
                        kv[0, place, :],
                        (((1,), (1,)), ((), ())),
                        preferred_element_type=jnp.float32,
                    )
                    + bias[...]
                )
                old = m_ref[head]
                new = jnp.maximum(old, jnp.max(s, axis=1, keepdims=True))
                m_ref[head] = new
                factor = jnp.exp2((old - new) * scale)
                w = jnp.exp2((s - jnp.tile(new, (1, 2 * rows // dim))) * scale)
                l_ref[head] = l_ref[head] * factor + jnp.sum(w, axis=1, keepdims=True)
                acc_ref[head] = acc_ref[head] * factor + jnp.dot(
                    w.astype(jnp.bfloat16), kv[1, place, :], preferred_element_type=jnp.float32
                )

    def step(i, carry):
        level = z - i
        arrived(2, level, level * 4 + 2 * y + 1 - c, partner)
        process(level * 2 + y)

        @pl.when(level > 0)
        def _():
            arrived(0, level - 1, (level - 1) * 4 + r, up)
            relay(level - 1)

        other = level * 4 + 2 * (1 - y) + c
        arrived(1, level, other, across)
        start(3, level, other, partner)

        @pl.when(i > 0)
        def _():
            arrived(3, level + 1, (level + 1) * 4 + 2 * (1 - y) + 1 - c, partner)
            process((level + 1) * 2 + 1 - y)

        return carry

    lax.fori_loop(0, z + 1, step, 0)
    arrived(3, 0, 2 * (1 - y) + 1 - c, partner)
    process(1 - y)

    for head in range(heads):
        o_ref[:, head * dim : (head + 1) * dim] = (acc_ref[head] / l_ref[head]).astype(o_ref.dtype)

    def finish(level, carry):
        block = level * 4 + r

        @pl.when(z < levels - 1)
        def _():
            sent(0, level, block, up)

        sent(1, level, block, across)
        sent(2, level, block, partner)
        sent(3, level, level * 4 + 2 * (1 - y) + c, partner)
        return carry

    lax.fori_loop(0, z + 1, finish, 0)


def solution(mesh):
    n = mesh.shape["ctx"]

    def on_device(queries, keys, values, doc_ids):
        rows, width = queries.shape
        dim = keys.shape[1]
        heads = width // dim
        levels = n // 4
        vmem = pl.BlockSpec(memory_space=pltpu.VMEM)
        anywhere = pl.BlockSpec(memory_space=pl.ANY)
        sems = pltpu.SemaphoreType.DMA((4, levels))
        return pl.pallas_call(
            functools.partial(kernel, n),
            out_shape=jax.ShapeDtypeStruct((rows, width), jnp.bfloat16),
            in_specs=[vmem, anywhere, anywhere, anywhere],
            out_specs=vmem,
            scratch_shapes=[
                pltpu.VMEM((2, n * rows, dim), jnp.bfloat16),
                pltpu.VMEM((n, 1, rows), jnp.int32),
                pltpu.VMEM((rows, 2 * rows), jnp.float32),
                pltpu.VMEM((heads, rows, dim), jnp.float32),
                pltpu.VMEM((heads, rows, dim), jnp.float32),
                pltpu.VMEM((heads, rows, dim), jnp.float32),
                pltpu.SemaphoreType.DMA((3,)),
                sems,
                sems,
                sems,
                sems,
            ],
            compiler_params=pltpu.CompilerParams(collective_id=0, has_side_effects=True),
        )(queries, keys, values, doc_ids.reshape(1, rows))

    spec = P(("groups", "ctx"), None)
    return jax.shard_map(
        on_device,
        mesh=mesh,
        in_specs=(spec, spec, spec, P(("groups", "ctx"))),
        out_specs=spec,
        check_vma=False,
    )
```

time: 164 us -> 30.5 us (0.19)
  waiting for transfers between devices: 59.8 us -> 0 us
  matrix products: 36.4 us -> 0 us
  Pallas kernels: 0 us -> 28.4 us
  other arithmetic: 25.3 us -> 0 us
  blocking collectives: 17.1 us -> 0 us
  between operations: 13.5 us -> 0.01 us
  loops' own time: 5.57 us -> 0 us
  local copies, waits for them, and re-layouts: 5.78 us -> 1.87 us
    all_gather x2 -> x0, waiting for transfers between devices: 58.4 us -> none  [the longest x1 39 us: on_device(): value_piece = lax.all_gather(values, 'ctx', axis=0, tiled=True)]
    dot_general x8 -> x0, matrix products: 36.4 us -> none  [the longest x4 19.3 us: attend_block(): jnp.dot(flat_weights, value_block, preferred_element_type=jnp.float32)]
    pallas_call x0 -> x1, Pallas kernels: none -> 28.4 us  [on_device(): pl.pallas_call(functools.partial(kernel, n), out_shape=jax.ShapeDtypeStru...]
    reduce_sum x4 -> x0, other arithmetic: 19.8 us -> none  [attend_block(): weight_sum = weight_sum * factor + jnp.sum(weights, axis=2)]
    all_gather x1 -> x0, blocking collectives: 17.1 us -> none  [on_device(): doc_piece = lax.all_gather(doc_ids, 'ctx', axis=0, tiled=True)]
    another operation x5 -> x0, loops' own time: 5.57 us -> none  [the longest x1 5.28 us: on_device(): state_all, unused = lax.scan(advance, state_all, stacked)]
    squeeze x2 -> x0, local copies, waits for them, and re-layouts: 2.55 us -> none  [on_device(): state_all, unused = lax.scan(advance, state_all, stacked)]
    unnamed x0 -> x1, local copies, waits for them, and re-layouts: none -> 1.87 us
  transfers between devices with their start and end apart: 2 -> 0, of which waited for: 2 -> 0; matrix products, arithmetic and copies ran while one was open for 2% -> 0% of each run, Pallas kernels for 0% -> 0%
where the time goes in v1:
time: 30.5 us; the launch traced here: 30.3 us
  Pallas kernels  28.4 us (93%)
  local copies, waits for them, and re-layouts  1.87 us (6%)
    pallas_call x1, Pallas kernels, on_device(): pl.pallas_call(functools.partial(kernel, n), out_shape=jax.ShapeDtypeStru...  28.4 us
    unnamed x1, local copies, waits for them, and re-layouts  1.87 us

profile of v1, /device:TPU:24, one launch (start us, length us, event | category | flops | bytes accessed | tf_op | source)
XLA Modules:
  0.0 30.3 jit_solution(9654584902034236654)
XLA Ops:
  0.0 28.4 %shard_map.46 = bf16[256,1024]{1,0:T(8,128)(2,1)} custom-call(bf16[256,1024]{1,0:T(8,128)(2,1)} %q_ref.1, bf16[256,128]{1,0:T(8,128)(2,1)} %k_hbm.1, bf16[256,128]{1,0:T(8,128)(2,1)} %v_hbm.1, s32[1,256]{1,0:T(1,128)} %bitcast.1), custom_call_target="tpu_custom_call" | custom-call | tf_op jit(solution)/shard_map/pallas_call | solution.py:219
  28.4 1.9 %copy.6 = bf16[256,1024]{1,0:T(8,128)(2,1)} copy(bf16[256,1024]{1,0:T(8,128)(2,1)} %shard_map.46) | data formatting | bytes 1048576

commit v2 on v1

v2 whole, which is shorter than its diff:
```python
import functools

import jax
import jax.numpy as jnp
from jax import lax
from jax.experimental import pallas as pl
from jax.experimental.pallas import tpu as pltpu
from jax.sharding import PartitionSpec as P

HIDDEN = -1e30
LOG2E = 1.4426950408889634
TILE_HEADS = 2


def kernel(
    n,
    q_hbm,
    k_hbm,
    v_hbm,
    d_hbm,
    o_hbm,
    q_ref,
    o_ref,
    kv,
    docs,
    bias,
    m_ref,
    acc_ref,
    qs,
    fill_sem,
    out_sem,
    send_kv,
    recv_kv,
    send_doc,
    recv_doc,
):
    rows, width = q_hbm.shape
    dim = k_hbm.shape[1]
    heads = width // dim
    levels = n // 4
    window = 3 * n // 4
    depth = (window + 3) // 4
    me = lax.axis_index("ctx")
    z = me // 4
    r = me % 4
    y = r // 2
    c = r % 2
    chip = me // 2
    up = me + 4
    across = z * 4 + (1 - y) * 2 + c
    partner = z * 4 + y * 2 + (1 - c)
    scale = dim ** (-0.5) * LOG2E
    keys_wide = 2 * rows

    def span(block):
        return pl.ds(pl.multiple_of(block * rows, rows), rows)

    fills = [
        pltpu.make_async_copy(k_hbm, kv.at[0, span(me), :], fill_sem.at[0]),
        pltpu.make_async_copy(v_hbm, kv.at[1, span(me), :], fill_sem.at[1]),
        pltpu.make_async_copy(d_hbm, docs.at[me], fill_sem.at[2]),
    ]
    for fill in fills:
        fill.start()
    query_fill = pltpu.make_async_copy(q_hbm, q_ref, fill_sem.at[3])
    query_fill.start()

    barrier = pltpu.get_barrier_semaphore()

    def greet(device):
        pl.semaphore_signal(
            barrier, inc=1, device_id={"ctx": device}, device_id_type=pl.DeviceIdType.MESH
        )

    greet(partner)
    greet(across)

    @pl.when(z > 0)
    def _():
        greet(me - 4)

    @pl.when(z < levels - 1)
    def _():
        greet(up)

    pl.semaphore_wait(barrier, 2 + jnp.minimum(z, 1) + jnp.minimum(levels - 1 - z, 1))

    def copies(stream, level, piece, block, device):
        made = [
            pltpu.make_async_remote_copy(
                src_ref=kv.at[piece, span(block), :],
                dst_ref=kv.at[piece, span(block), :],
                send_sem=send_kv.at[stream, level, piece],
                recv_sem=recv_kv.at[stream, level, piece],
                device_id={"ctx": device},
                device_id_type=pl.DeviceIdType.MESH,
            )
        ]
        if piece == 0:
            made.append(
                pltpu.make_async_remote_copy(
                    src_ref=docs.at[block],
                    dst_ref=docs.at[block],
                    send_sem=send_doc.at[stream, level],
                    recv_sem=recv_doc.at[stream, level],
                    device_id={"ctx": device},
                    device_id_type=pl.DeviceIdType.MESH,
                )
            )
        return made

    def start(*where):
        for copy in copies(*where):
            copy.start()

    def arrived(*where):
        for copy in copies(*where):
            copy.wait_recv()

    def sent(*where):
        for copy in copies(*where):
            copy.wait_send()

    def needs(some_chip, chunk):
        return (chunk <= some_chip) & (2 * chunk + 1 >= 2 * some_chip - window)

    def climbs(level):
        return (z < levels - 1) & (z - level < depth)

    def crosses(level):
        return needs(2 * z + 1 - y, 2 * level + y)

    def crossed(level):
        return needs(chip, 2 * level + 1 - y)

    def relay(level, piece):
        block = level * 4 + r

        @pl.when(climbs(level))
        def _():
            start(0, level, piece, block, up)

        @pl.when(crosses(level))
        def _():
            start(1, level, piece, block, across)

        start(2, level, piece, block, partner)

    for fill in fills[:1] + fills[2:]:
        fill.wait()
    relay(z, 0)
    fills[1].wait()
    relay(z, 1)

    lane = lax.broadcasted_iota(jnp.int32, (rows, dim), 1)
    row_id = me * rows + lax.broadcasted_iota(jnp.int32, (rows, dim), 0)
    doc_col = jnp.broadcast_to(docs[me], (dim, rows)).T
    query_marks = jnp.where(lane == doc_col, 0.0, HIDDEN).astype(jnp.bfloat16)
    query_fill.wait()
    for head in range(heads):
        here = slice(head * rows, (head + 1) * rows)
        qs[here, :dim] = q_ref[:, head * dim : (head + 1) * dim]
        qs[here, dim:] = query_marks

    def attend(chunk, first, hooks):
        place = pl.ds(pl.multiple_of(chunk * keys_wide, keys_wide), keys_wide)
        marks = []
        for half in range(2):
            key_col = jnp.broadcast_to(docs[chunk * 2 + half], (dim, rows)).T
            marks.append(jnp.where(lane == key_col, 1.0, 0.0).astype(jnp.bfloat16))
        k_chunk = jnp.concatenate([kv[0, place, :], jnp.concatenate(marks, axis=0)], axis=1)
        v_chunk = jnp.concatenate(
            [kv[1, place, :], jnp.ones((keys_wide, dim), jnp.bfloat16)], axis=1
        )
        if first:
            for part in range(keys_wide // dim):
                key_id = chunk * keys_wide + part * dim + lane
                bias[:, part * dim : (part + 1) * dim] = jnp.where(key_id <= row_id, 0.0, HIDDEN)
        tile_rows = TILE_HEADS * rows

        def scores(tile):
            return lax.dot_general(
                qs[tile * tile_rows : (tile + 1) * tile_rows, :],
                k_chunk,
                (((1,), (1,)), ((), ())),
                preferred_element_type=jnp.float32,
            )

        tiles = heads // TILE_HEADS
        following = scores(0)
        for tile in range(tiles):
            s = following
            if tile + 1 < tiles:
                following = scores(tile + 1)
            here = slice(tile * tile_rows, (tile + 1) * tile_rows)
            if first:
                s = s + jnp.concatenate([bias[...]] * TILE_HEADS, axis=0)
            new = jnp.max(s, axis=1, keepdims=True)
            if first:
                new = jnp.broadcast_to(new, (tile_rows, dim))
            else:
                old = m_ref[here]
                new = jnp.maximum(old, new)
            m_ref[here] = new
            w = jnp.exp2((s - jnp.tile(new, (1, keys_wide // dim))) * scale)
            part = jnp.dot(w.astype(jnp.bfloat16), v_chunk, preferred_element_type=jnp.float32)
            if first:
                acc_ref[here] = part
            else:
                acc_ref[here] = (
                    acc_ref[here] * jnp.tile(jnp.exp2((old - new) * scale), (1, 2)) + part
                )
            if tile < len(hooks):
                hooks[tile]()

    def process(chunk, hooks=()):
        needed = (chunk <= chip) & (chunk * 2 + 1 >= me - window)

        @pl.when(needed)
        def _():
            attend(chunk, False, hooks)

        if hooks:

            @pl.when(jnp.logical_not(needed))
            def _():
                for hook in hooks:
                    hook()

    def from_below(level, piece):
        def hook():
            @pl.when(level > jnp.maximum(z - depth, 0))
            def _():
                arrived(0, level - 1, piece, (level - 1) * 4 + r, up)
                relay(level - 1, piece)

        return hook

    def from_across(level, piece):
        block = level * 4 + 2 * (1 - y) + c

        def hook():
            @pl.when(crossed(level))
            def _():
                arrived(1, level, piece, block, across)
                start(3, level, piece, block, partner)

        return hook

    def own_column(level):
        for piece in range(2):
            arrived(2, level, piece, level * 4 + 2 * y + 1 - c, partner)

    def other_column(level):
        @pl.when(crossed(level))
        def _():
            for piece in range(2):
                arrived(3, level, piece, level * 4 + 2 * (1 - y) + 1 - c, partner)

    def hooks_of(level):
        return (
            from_below(level, 0),
            from_across(level, 0),
            from_below(level, 1),
            from_across(level, 1),
        )

    own_column(z)
    attend(chip, True, hooks_of(z))

    def step(i, carry):
        level = z - i
        own_column(level)
        process(level * 2 + y, hooks_of(level))
        other_column(level + 1)
        process((level + 1) * 2 + 1 - y)
        return carry

    last = jnp.minimum(z, depth)
    lax.fori_loop(1, last + 1, step, 0)
    other_column(z - last)
    process((z - last) * 2 + 1 - y)

    def out_copy(head):
        cols = slice(head * dim, (head + 1) * dim)
        return pltpu.make_async_copy(o_ref.at[:, cols], o_hbm.at[:, cols], out_sem.at[head])

    for head in range(heads):
        here = slice(head * rows, (head + 1) * rows)
        o_ref[:, head * dim : (head + 1) * dim] = (acc_ref[here, :dim] / acc_ref[here, dim:]).astype(
            o_ref.dtype
        )
        out_copy(head).start()

    def finish(i, carry):
        level = z - i
        block = level * 4 + r
        for piece in range(2):

            @pl.when(climbs(level))
            def _():
                sent(0, level, piece, block, up)

            @pl.when(crosses(level))
            def _():
                sent(1, level, piece, block, across)

            sent(2, level, piece, block, partner)

            @pl.when(crossed(level))
            def _():
                sent(3, level, piece, level * 4 + 2 * (1 - y) + c, partner)

        return carry

    lax.fori_loop(0, last + 1, finish, 0)
    for head in range(heads):
        out_copy(head).wait()


def solution(mesh):
    n = mesh.shape["ctx"]

    def on_device(queries, keys, values, doc_ids):
        rows, width = queries.shape
        dim = keys.shape[1]
        heads = width // dim
        levels = n // 4
        anywhere = pl.BlockSpec(memory_space=pl.ANY)
        piece_sems = pltpu.SemaphoreType.DMA((4, levels, 2))
        doc_sems = pltpu.SemaphoreType.DMA((4, levels))
        return pl.pallas_call(
            functools.partial(kernel, n),
            out_shape=jax.ShapeDtypeStruct((rows, width), jnp.bfloat16),
            in_specs=[anywhere] * 4,
            out_specs=anywhere,
            scratch_shapes=[
                pltpu.VMEM((rows, width), jnp.bfloat16),
                pltpu.VMEM((rows, width), jnp.bfloat16),
                pltpu.VMEM((2, n * rows, dim), jnp.bfloat16),
                pltpu.VMEM((n, 1, rows), jnp.int32),
                pltpu.VMEM((rows, 2 * rows), jnp.float32),
                pltpu.VMEM((heads * rows, dim), jnp.float32),
                pltpu.VMEM((heads * rows, 2 * dim), jnp.float32),
                pltpu.VMEM((heads * rows, 2 * dim), jnp.bfloat16),
                pltpu.SemaphoreType.DMA((4,)),
                pltpu.SemaphoreType.DMA((heads,)),
                piece_sems,
                piece_sems,
                doc_sems,
                doc_sems,
            ],
            compiler_params=pltpu.CompilerParams(collective_id=0, has_side_effects=True),
        )(queries, keys, values, doc_ids.reshape(1, rows))

    spec = P(("groups", "ctx"), None)
    return jax.shard_map(
        on_device,
        mesh=mesh,
        in_specs=(spec, spec, spec, P(("groups", "ctx"))),
        out_specs=spec,
        check_vma=False,
    )
```

time: 30.5 us -> 24.7 us (0.81)
  Pallas kernels: 28.4 us -> 22.6 us
    pallas_call x1, Pallas kernels: 28.4 us -> 22.6 us  [on_device(): pl.pallas_call(functools.partial(kernel, n), out_shape=jax.ShapeDtypeStru...]
where the time goes in v2:
time: 24.7 us; the launch traced here: 24.5 us
  Pallas kernels  22.6 us (91%)
  local copies, waits for them, and re-layouts  1.87 us (8%)
    pallas_call x1, Pallas kernels, on_device(): pl.pallas_call(functools.partial(kernel, n), out_shape=jax.ShapeDtypeStru...  22.6 us
    unnamed x1, local copies, waits for them, and re-layouts  1.87 us

profile of v2, /device:TPU:24, one launch (start us, length us, event | category | flops | bytes accessed | tf_op | source)
XLA Modules:
  0.0 24.5 jit_solution(12245234281521757129)
XLA Ops:
  0.0 22.6 %shard_map.46 = bf16[256,1024]{1,0:T(8,128)(2,1)} custom-call(bf16[256,1024]{1,0:T(8,128)(2,1)} %q_hbm.1, bf16[256,128]{1,0:T(8,128)(2,1)} %k_hbm.1, bf16[256,128]{1,0:T(8,128)(2,1)} %v_hbm.1, s32[1,256]{1,0:T(1,128)} %bitcast.1), custom_call_target="tpu_custom_call" | custom-call | tf_op jit(solution)/shard_map/pallas_call | solution.py:332
  22.6 1.9 %copy.6 = bf16[256,1024]{1,0:T(8,128)(2,1)} copy(bf16[256,1024]{1,0:T(8,128)(2,1)} %shard_map.46) | data formatting | bytes 1048576

commit v3 on v2

--- a/solution.py
+++ b/solution.py
@@ -350,8 +350,8 @@
                 doc_sems,
                 doc_sems,
             ],
-            compiler_params=pltpu.CompilerParams(collective_id=0, has_side_effects=True),
-        )(queries, keys, values, doc_ids.reshape(1, rows))
+            compiler_params=pltpu.CompilerParams(collective_id=0, has_side_effects=True, vmem_limit_bytes=16 * 1024 * 1024),
+        )(*[pltpu.with_memory_space_constraint(a, pltpu.HBM) for a in (queries, keys, values, doc_ids.reshape(1, rows))])
 
     spec = P(("groups", "ctx"), None)
     return jax.shard_map(

time: 24.7 us -> 23.3 us (0.943)
  local copies, waits for them, and re-layouts: 1.87 us -> 0.8 us
  Pallas kernels: 22.6 us -> 22.3 us
    unnamed x1, local copies, waits for them, and re-layouts: 1.87 us -> 0.8 us
    pallas_call x1, Pallas kernels: 22.6 us -> 22.3 us  [on_device(): pl.pallas_call(functools.partial(kernel, n), out_shape=jax.ShapeDtypeStru...]
where the time goes in v3:
time: 23.3 us; the launch traced here: 23.1 us
  Pallas kernels  22.3 us (96%)
  local copies, waits for them, and re-layouts  0.8 us (3%)
    pallas_call x1, Pallas kernels, on_device(): pl.pallas_call(functools.partial(kernel, n), out_shape=jax.ShapeDtypeStru...  22.3 us
    unnamed x1, local copies, waits for them, and re-layouts  0.8 us

profile of v3, /device:TPU:24, one launch (start us, length us, event | category | flops | bytes accessed | tf_op | source)
XLA Modules:
  0.0 23.1 jit_solution(11836276288144211689)
XLA Ops:
  0.0 22.3 %shard_map.46 = bf16[256,1024]{1,0:T(8,128)(2,1)S(1)} custom-call(bf16[256,1024]{1,0:T(8,128)(2,1)} %q_hbm.1, bf16[256,128]{1,0:T(8,128)(2,1)} %k_hbm.1, bf16[256,128]{1,0:T(8,128)(2,1)} %v_hbm.1, s32[1,256]{1,0:T(1,128)} %bitcast.1), custom_call_target="tpu_custom_call" | custom-call | tf_op jit(solution)/shard_map/pallas_call | solution.py:332
  22.3 0.8 %copy.6 = bf16[256,1024]{1,0:T(8,128)(2,1)} copy(bf16[256,1024]{1,0:T(8,128)(2,1)S(1)} %shard_map.46) | data formatting | bytes 1048576

commit v4 on v3

--- a/solution.py
+++ b/solution.py
@@ -260,8 +260,8 @@
     def hooks_of(level):
         return (
             from_below(level, 0),
+            from_below(level, 1),
             from_across(level, 0),
-            from_below(level, 1),
             from_across(level, 1),
         )
 

time: 23.3 us -> 22.5 us (0.966)
  Pallas kernels: 22.3 us -> 21.5 us
    pallas_call x1, Pallas kernels: 22.3 us -> 21.5 us  [on_device(): pl.pallas_call(functools.partial(kernel, n), out_shape=jax.ShapeDtypeStru...]
where the time goes in v4:
time: 22.5 us; the launch traced here: 22.3 us
  Pallas kernels  21.5 us (96%)
  local copies, waits for them, and re-layouts  0.8 us (4%)
    pallas_call x1, Pallas kernels, on_device(): pl.pallas_call(functools.partial(kernel, n), out_shape=jax.ShapeDtypeStru...  21.5 us
    unnamed x1, local copies, waits for them, and re-layouts  0.8 us

profile of v4, /device:TPU:24, one launch (start us, length us, event | category | flops | bytes accessed | tf_op | source)
XLA Modules:
  0.0 22.3 jit_solution(15059823639331218540)
XLA Ops:
  0.0 21.5 %shard_map.46 = bf16[256,1024]{1,0:T(8,128)(2,1)S(1)} custom-call(bf16[256,1024]{1,0:T(8,128)(2,1)} %q_hbm.1, bf16[256,128]{1,0:T(8,128)(2,1)} %k_hbm.1, bf16[256,128]{1,0:T(8,128)(2,1)} %v_hbm.1, s32[1,256]{1,0:T(1,128)} %bitcast.1), custom_call_target="tpu_custom_call" | custom-call | tf_op jit(solution)/shard_map/pallas_call | solution.py:332
  21.5 0.8 %copy.6 = bf16[256,1024]{1,0:T(8,128)(2,1)} copy(bf16[256,1024]{1,0:T(8,128)(2,1)S(1)} %shard_map.46) | data formatting | bytes 1048576
